TPU v7x, 512 devices: a whole 4x4x16 slice. The times are simulated.
512 devices in a mesh: row: 16 (over z), col: 16 (over y, x_lo, core), rep: 2 (over x_hi).
Axes of the slice: x: 4 (x_hi: 2, x_lo: 2; x = x_hi * 2 + x_lo), y: 4, z: 16, core: 2. Of those that a mesh axis runs over, the one named last changes fastest.
Arguments:
- tokens: bfloat16 [8192, 8192], P(('row', 'rep'), 'col'), may hold values from -6 to 6
- output_gradient: bfloat16 [8192, 8192], P(('row', 'rep'), 'col'), may hold values from -0.15625 to 0.15625
- master_weight: float32 [8192, 8192], P('row', 'col'), may hold values from -0.0625 to 0.0625
- old_down: float32 [8192, 128], P('row'), may hold values from -0.0625 to 0.0625
- old_up: float32 [128, 8192], P(None, 'col'), may hold values from -5 to 5
- fresh_down: float32 [8192, 128], P('col'), may hold values from -0.0625 to 0.0625
- fresh_up: float32 [128, 8192], P(None, 'col'), may hold values from -0.5 to 0.5
- m_down: float32 [8192, 128], P(('col', 'row')), may hold values from -6 to 6
- v_down: float32 [8192, 128], P(('col', 'row')), may hold values from 1 to 16
- m_up: float32 [128, 8192], P(None, ('col', 'row')), may hold values from -4 to 4
- v_up: float32 [128, 8192], P(None, ('col', 'row')), may hold values from 0.015625 to 0.25
- keep_down: int32 [512], P(('col', 'row')), may hold values 0 or 1
- keep_up: int32 [512], P(('col', 'row')), may hold values 0 or 1
Outputs:
- merged_weight: float32 [8192, 8192], P('row', 'col')
- w_copy: bfloat16 [8192, 8192], P('row', 'col')
- outputs: bfloat16 [8192, 8192], P(('row', 'rep'), 'col')
- m_down_new: float32 [8192, 128], P(('col', 'row'))
- v_down_new: float32 [8192, 128], P(('col', 'row'))
- m_up_new: float32 [128, 8192], P(None, ('col', 'row'))
- v_up_new: float32 [128, 8192], P(None, ('col', 'row'))
All inputs are finite; a program needn't handle non-finite values. No bound on the sum of `keep_down` or of `keep_up` on one device may be relied on, other than what follows from the above.
Results may differ from a plain program's by a relative error of at most 0.0051.
Values may be sent and summed in bfloat16 or wider, within the bound.
A program may use at most 64 MiB of HBM per device.

v0:
```python
import jax
import jax.numpy as jnp
from jax import lax
from jax.sharding import Mesh
from jax.sharding import PartitionSpec as P

BLOCK = 16
COL = ("col_0", "col_1", "col_2")
COL_ROW = ("col_0", "col_1", "col_2", "row")


adapter_scale = 0.25
beta_one = 0.9
beta_two = 0.95


def split_up(shard, dim, length):
    before, after = (shard.shape[:dim], shard.shape[dim + 1 :])
    return jnp.moveaxis(shard.reshape(*before, length, -1, *after), dim, 0)


def sent_and_summed(shard, axis, dim):
    tiles = split_up(shard, dim, lax.axis_size(axis))
    arrived = lax.all_to_all(tiles, axis, split_axis=0, concat_axis=0, tiled=True)
    return arrived.sum(axis=0)


def padded_to(lines, length):
    spare = -len(lines) % length
    return jnp.pad(lines, [(0, spare)] + [(0, 0)] * (lines.ndim - 1))


def copy_for_each(shard, axis):
    length = lax.axis_size(axis)
    return lax.all_to_all(
        jnp.broadcast_to(shard[None], (length, *shard.shape)), axis, 0, 0, tiled=True
    )


def in_order(tiles, dim):
    dims = list(tiles.shape[1:])
    dims[dim] *= tiles.shape[0]
    return jnp.moveaxis(tiles, 0, dim).reshape(dims)


def gathered_copies(shard, axis, dim):
    tiles = copy_for_each(shard, axis)
    return in_order(tiles, dim)


def total_of(shard, axes):
    own = sent_and_summed(padded_to(shard, lax.axis_size(axes)), axes, 0)
    whole = gathered_copies(own, axes, 0)
    return whole[: len(shard)].reshape(shard.shape)


def in_one(arrays, axis):
    ravelled, at, done = (jnp.concatenate([a.reshape(-1) for a in arrays]), 0, [])
    so_far = total_of(ravelled, axis)
    for a in arrays:
        done.append(so_far[at : at + a.size].reshape(a.shape))
        at += a.size
    return tuple(done)


def gathered_by_axis(shard, axes, dim):
    far, near = axes
    first = copy_for_each(shard, far)
    tiles = jnp.swapaxes(copy_for_each(first, near), 0, 1)
    return in_order(tiles.reshape(-1, *shard.shape), dim)


def sum_at_owner(shard, axis, dim):
    length = lax.axis_size(axis)
    tiles = lax.all_to_all(split_up(shard, dim, length), axis, 0, 0, tiled=True)
    return jnp.sum(tiles.astype(jnp.float32), axis=0)


def sent_together(arrays, axis, dim, along):
    both = jnp.concatenate(arrays, axis=along)
    filled, at, done = (sum_at_owner(both, axis, dim), 0, [])
    for a in arrays:
        done.append(lax.slice_in_dim(filled, at, at + a.shape[along], axis=along))
        at += a.shape[along]
    return tuple(done)


def taken_together(shard, axis):
    return copy_for_each(shard, axis).astype(jnp.float32).sum(axis=0)


def adam_moments(first_moment, second_moment, keep_scale, gradient):
    first_new = beta_one * keep_scale * first_moment + (1.0 - beta_one) * gradient
    second_new = beta_two * keep_scale * second_moment + (1.0 - beta_two) * gradient * gradient
    return (first_new, second_new)


def body(
    tokens,
    output_gradient,
    master_weight,
    old_down,
    old_up,
    fresh_down,
    fresh_up,
    m_down,
    v_down,
    m_up,
    v_up,
    keep_down,
    keep_up,
):
    previous_product = jnp.dot(
        old_down, old_up, precision=lax.Precision.HIGHEST, preferred_element_type=jnp.float32
    )
    merged_weight = master_weight + adapter_scale * previous_product
    w_copy = merged_weight.astype(jnp.bfloat16)
    down_cast = fresh_down.astype(jnp.bfloat16)
    up_cast = fresh_up.astype(jnp.bfloat16)
    partial_hidden = jnp.dot(tokens, down_cast, preferred_element_type=jnp.float32)
    partial_back = lax.dot_general(
        output_gradient, up_cast, (((1,), (1,)), ((), ())), preferred_element_type=jnp.float32
    )
    hidden_sum, back_sum = in_one((partial_hidden, partial_back), COL)
    hidden_rows = hidden_sum.astype(jnp.bfloat16)
    backward_pass = back_sum.astype(jnp.bfloat16)
    gathered = gathered_by_axis(tokens, (("col_0", "col_1"), "col_2"), 1)
    adapter_product = jnp.dot(
        gathered,
        lax.all_gather(w_copy, "row", axis=0, tiled=True),
        preferred_element_type=jnp.float32,
    )
    adapter_branch = jnp.dot(hidden_rows, up_cast, preferred_element_type=jnp.float32)
    outputs = (adapter_product + adapter_scale * adapter_branch).astype(jnp.bfloat16)
    down_gradient = adapter_scale * lax.dot_general(
        tokens, backward_pass, (((0,), (0,)), ((), ())), preferred_element_type=jnp.float32
    )
    up_gradient = adapter_scale * lax.dot_general(
        output_gradient, hidden_rows, (((0,), (0,)), ((), ())), preferred_element_type=jnp.float32
    )
    share_down, share_up = sent_together(
        (down_gradient.astype(jnp.bfloat16), up_gradient.astype(jnp.bfloat16)), "row", 0, 1
    )
    down_rows, up_rows = (
        taken_together(share_down.astype(jnp.bfloat16), "rep").astype(jnp.float32),
        taken_together(share_up.astype(jnp.bfloat16), "rep").astype(jnp.float32),
    )
    keep_rows = jnp.repeat(keep_down.astype(jnp.float32), BLOCK)[:, None]
    keep_cols = jnp.repeat(keep_up.astype(jnp.float32), BLOCK)[None, :]
    m_down_new, v_down_new = adam_moments(m_down, v_down, keep_rows, down_rows)
    m_up_new, v_up_new = adam_moments(m_up, v_up, keep_cols, up_rows.T)
    return (merged_weight, w_copy, outputs, m_down_new, v_down_new, m_up_new, v_up_new)


def solution(mesh):
    finer = Mesh(
        mesh.devices.reshape(mesh.shape["row"], 4, 2, 2, mesh.shape["rep"]),
        ("row", "col_0", "col_1", "col_2", "rep"),
    )
    return jax.shard_map(
        body,
        mesh=finer,
        in_specs=(
            P(("row", "rep"), COL),
            P(("row", "rep"), COL),
            P("row", COL),
            P("row", None),
            P(None, COL),
            P(COL, None),
            P(None, COL),
            P(COL_ROW, None),
            P(COL_ROW, None),
            P(None, COL_ROW),
            P(None, COL_ROW),
            P(COL_ROW),
            P(COL_ROW),
        ),
        out_specs=(
            P("row", COL),
            P("row", COL),
            P(("row", "rep"), COL),
            P(COL_ROW, None),
            P(COL_ROW, None),
            P(None, COL_ROW),
            P(None, COL_ROW),
        ),
        check_vma=False,
    )
```

profile of v0, /device:TPU:1, one launch (start us, length us, event | category | flops | bytes accessed | tf_op | source)
XLA Modules:
  0.0 153.1 jit_solution(11111849858414570460)
XLA Ops:
  7.3 1.0 copy-done
  8.3 3.5 %fusion.16 = (bf16[512,512]{1,0:T(8,128)(2,1)}, f32[512,512]{1,0:T(8,128)}) fusion(f32[512,512]{1,0:T(8,128)} %param.15, f32[512,128]{1,0:T(8,128)S(1)} %copy-done, f32[128,512]{1,0:T(8,128)} %param.17), kind=kOutput, calls=%fused_computation.35 | convolution fusion | flops 403439616 | bytes 3145728 | tf_op jit(solution)/shard_map/dot_general | solution.py:113
  11.8 1.3 fusion.10
  13.1 0.2 fusion.7
  13.4 0.3 all_to_all.27
  13.6 16.5 %all_to_all.40 = f32[16,1,4096]{2,1,0:T(1,128)S(1)} all-to-all(f32[16,1,4096]{2,1,0:T(1,128)S(1)} %all_to_all.27), channel_id=1, replica_groups=mesh['row'=16,'col_0'=4,'col_1'=2,'col_2'=2,'rep'=2] {'col_0','col_1','c..., dimensions={0} | all-to-all | bytes 524288 | tf_op jit(solution)/shard_map/all_to_all | solution.py:24
  30.1 0.2 reduce_sum.36
  30.3 0.2 broadcast_in_dim.20
  30.5 0.5 broadcast.52
  31.1 1.4 reduce.6
  32.5 9.6 %all_to_all.41 = bf16[16,2,2048]{2,1,0:T(2,128)(2,1)S(1)} all-to-all(bf16[16,2,2048]{2,1,0:T(2,128)(2,1)S(1)} %reshape.96), channel_id=1, replica_groups=mesh['row'=16,'col_0'=4,'col_1'=2,'col_2'=2,'rep'=2] {'col_0','col_1','c..., dimensions={0} | all-to-all | bytes 262144 | tf_op jit(solution)/shard_map/all_to_all | solution.py:35
  42.1 0.1 reshape.97
  42.2 0.5 slice_reduce_fusion
  42.8 0.2 fusion.5
  43.1 0.2 fusion.6
  43.4 0.1 copy.34
  43.5 31.2 %all_to_all.42 = bf16[16,32,256]{2,1,0:T(8,128)(2,1)S(1)} all-to-all(bf16[16,32,256]{2,1,0:T(8,128)(2,1)S(1)} %bitcast.31), channel_id=1, replica_groups=mesh['row'=16,'col_0'=4,'col_1'=2,'col_2'=2,'rep'=2] {'row'}, dimensions={0} | all-to-all | bytes 524288 | tf_op jit(solution)/shard_map/all_to_all | solution.py:75
  74.8 7.8 %all_to_all.43 = bf16[2,32,128]{2,1,0:T(8,128)(2,1)S(1)} all-to-all(bf16[2,32,128]{2,1,0:T(8,128)(2,1)S(1)} %broadcast_in_dim.44), channel_id=1, replica_groups=mesh['row'=16,'col_0'=4,'col_1'=2,'col_2'=2,'rep'=2] {'rep'}, dimensions={0} | all-to-all | bytes 32768 | tf_op jit(solution)/shard_map/all_to_all | solution.py:35
  82.5 6.6 %all_to_all.44 = bf16[2,32,128]{2,1,0:T(8,128)(2,1)S(1)} all-to-all(bf16[2,32,128]{2,1,0:T(8,128)(2,1)S(1)} %broadcast_in_dim.47), channel_id=1, replica_groups=mesh['row'=16,'col_0'=4,'col_1'=2,'col_2'=2,'rep'=2] {'rep'}, dimensions={0} | all-to-all | bytes 32768 | tf_op jit(solution)/shard_map/all_to_all | solution.py:35
  89.1 1.6 %broadcast_in_dim.18 = bf16[8,256,512]{2,1,0:T(8,128)(2,1)} broadcast(bf16[256,512]{1,0:T(8,128)(2,1)S(1)} %copy-done.1), dimensions={1,2} | broadcast | bytes 2359296 | tf_op jit(solution)/shard_map/broadcast_in_dim | solution.py:36
  90.7 3.6 %all-to-all-start = ((bf16[8,256,512]{2,1,0:T(8,128)(2,1)}), bf16[8,256,512]{2,1,0:T(8,128)(2,1)S(1)}, u32[]{:S(2)}, u32[]{:S(2)}) async-start(bf16[8,256,512]{2,1,0:T(8,128)(2,1)} %broadcast_in_dim.18), calls=%async_computation | async-start | bytes 4194304 | tf_op jit(solution)/shard_map/all_to_all | solution.py:35
  94.6 0.1 mul.144
  95.0 0.7 fusion.12
  95.7 0.7 fusion.13
  96.4 18.5 %all-to-all-done = bf16[8,256,512]{2,1,0:T(8,128)(2,1)S(1)} async-done(((bf16[8,256,512]{2,1,0:T(8,128)(2,1)}), bf16[8,256,512]{2,1,0:T(8,128)(2,1)S(1)}, u32[]{:S(2)}, u32[]{:S(2)}) %all-to-all-start) | async-done | bytes 2097184 | tf_op jit(solution)/shard_map/all_to_all | solution.py:35
  114.8 0.4 broadcast_in_dim.19
  115.3 14.1 %all_to_all.45 = bf16[2,8,256,512]{3,2,1,0:T(8,128)(2,1)S(1)} all-to-all(bf16[2,8,256,512]{3,2,1,0:T(8,128)(2,1)S(1)} %broadcast_in_dim.19), channel_id=1, replica_groups=mesh['row'=16,'col_0'=4,'col_1'=2,'col_2'=2,'rep'=2] {'col_2'}, dimensions={0} | all-to-all | bytes 8388608 | tf_op jit(solution)/shard_map/all_to_all | solution.py:35
  129.4 2.4 %copy.31 = bf16[2,8,256,512]{3,2,0,1:T(8,128)(2,1)} copy(bf16[2,8,256,512]{3,2,1,0:T(8,128)(2,1)S(1)} %all_to_all.45) | data formatting | bytes 8388608 | tf_op jit(solution)/shard_map/all_to_all | solution.py:35
  131.8 6.4 %copy.32 = bf16[256,16,512]{0,2,1:T(8,128)(2,1)} copy(bf16[256,16,512]{2,0,1:T(8,128)(2,1)} %bitcast.30) | data formatting | bytes 8388608 | tf_op jit(solution)/shard_map/transpose | solution.py:43
  138.1 7.0 %convolution_bitcast_fusion = f32[256,512]{0,1:T(8,128)S(1)} fusion(bf16[8192,512]{1,0:T(8,128)(2,1)} %all-gather.2.cloned.1.call-done, bf16[256,8192]{0,1:T(8,128)(2,1)} %bitcast.29), kind=kOutput, calls=%fused_computation.4 | convolution fusion | flops 2147483648 | bytes 13107200 | tf_op jit(solution)/shard_map/dot_general | solution.py:128
  145.1 0.3 fusion.2
  145.4 0.8 copy.35
  (46 shorter events, 1.0 us)
Async XLA Ops:
  7.2 1.1 copy-start
  7.2 35.7 %copy-start.3 = (bf16[256,512]{1,0:T(8,128)(2,1)S(1)}, bf16[256,512]{1,0:T(8,128)(2,1)}, u32[]{:S(2)}) copy-start(bf16[256,512]{1,0:T(8,128)(2,1)} %param.14) | copy-start | bytes 786436
  7.2 5.9 %copy-start.1 = (bf16[256,512]{1,0:T(8,128)(2,1)S(1)}, bf16[256,512]{1,0:T(8,128)(2,1)}, u32[]{:S(2)}) copy-start(bf16[256,512]{1,0:T(8,128)(2,1)} %param.13) | copy-start | bytes 786436
  7.2 5.9 %copy-start.4 = (f32[512,128]{1,0:T(8,128)S(1)}, f32[512,128]{1,0:T(8,128)}, u32[]{:S(2)}) copy-start(f32[512,128]{1,0:T(8,128)} %param.18) | copy-start | bytes 786436
  7.2 130.9 %all-gather.2.cloned.1.call-start = ((), (), s32[]{:S(2)}) async-start(), calls=%async_computation.7 | async-start | bytes 8912896 | tf_op jit(solution)/shard_map/all_gather | solution.py:130
  43.3 51.0 %copy-start.9 = (s32[2]{0:T(128)S(1)}, s32[2]{0:T(128)}, u32[]{:S(2)}) copy-start(s32[2]{0:T(128)} %param.24) | copy-start | bytes 28
  43.3 51.4 %copy-start.10 = (s32[2]{0:T(128)S(1)}, s32[2]{0:T(128)}, u32[]{:S(2)}) copy-start(s32[2]{0:T(128)} %param.25) | copy-start | bytes 28
  43.3 51.6 %copy-start.5 = (f32[32,128]{1,0:T(8,128)S(1)}, f32[32,128]{1,0:T(8,128)}, u32[]{:S(2)}) copy-start(f32[32,128]{1,0:T(8,128)} %param.21) | copy-start | bytes 49156
  43.3 51.6 %copy-start.6 = (f32[32,128]{1,0:T(8,128)S(1)}, f32[32,128]{1,0:T(8,128)}, u32[]{:S(2)}) copy-start(f32[32,128]{1,0:T(8,128)} %param.20) | copy-start | bytes 49156
  43.3 52.3 %copy-start.7 = (f32[128,32]{0,1:T(8,128)S(1)}, f32[128,32]{0,1:T(8,128)}, u32[]{:S(2)}) copy-start(f32[128,32]{0,1:T(8,128)} %param.23) | copy-start | bytes 49156
  43.4 52.3 %copy-start.8 = (f32[128,32]{0,1:T(8,128)S(1)}, f32[128,32]{0,1:T(8,128)}, u32[]{:S(2)}) copy-start(f32[128,32]{0,1:T(8,128)} %param.22) | copy-start | bytes 49156
  90.7 24.1 %all-to-all-start = ((bf16[8,256,512]{2,1,0:T(8,128)(2,1)}), bf16[8,256,512]{2,1,0:T(8,128)(2,1)S(1)}, u32[]{:S(2)}, u32[]{:S(2)}) async-start(bf16[8,256,512]{2,1,0:T(8,128)(2,1)} %broadcast_in_dim.18), calls=%async_computation | async-start | bytes 4194304 | tf_op jit(solution)/shard_map/all_to_all | solution.py:35
  138.1 7.0 %copy-start.2 = (f32[128,512]{1,0:T(8,128)S(1)}, f32[128,512]{1,0:T(8,128)}, u32[]{:S(2)}) copy-start(f32[128,512]{1,0:T(8,128)} %param.19) | copy-start | bytes 786436
Sparse Core Ops, SparseCore 0:
  11.9 122.2 all-gather.1
where the time goes:
time: 154 us; the launch traced here: 153 us
  blocking collectives  85.7 us (56%)
  waiting for transfers between devices  18.5 us (12%)
  local copies, waits for them, and re-layouts  15.3 us (10%)
  between operations  14.4 us (9%)
  matrix products  12.6 us (8%)
  starting transfers between devices  3.64 us (2%)
  other arithmetic  3.04 us (2%)
    all_to_all x4, blocking collectives, copy_for_each(): lax.all_to_all(jnp.broadcast_to(shard[None], (length, *shard.shape)), axi...  38 us
    all_to_all x1, blocking collectives, sum_at_owner(): tiles = lax.all_to_all(split_up(shard, dim, length), axis, 0, 0, tiled=True)  31.2 us
    all_to_all x1, waiting for transfers between devices, copy_for_each(): lax.all_to_all(jnp.broadcast_to(shard[None], (length, *shard.shape)), axi...  18.5 us
    all_to_all x1, blocking collectives, sent_and_summed(): lax.all_to_all(tiles, axis, split_axis=0, concat_axis=0, tiled=True)  16.5 us
    dot_general x1, matrix products, body(): jnp.dot(gathered, lax.all_gather(w_copy, 'row', axis=0, tiled=True), pref...  6.98 us
    transpose x1, local copies, waits for them, and re-layouts, in_order(): return jnp.moveaxis(tiles, 0, dim).reshape(dims)  6.36 us
    all_to_all x1, starting transfers between devices, copy_for_each(): lax.all_to_all(jnp.broadcast_to(shard[None], (length, *shard.shape)), axi...  3.6 us
    dot_general x1, matrix products, body(): jnp.dot(old_down, old_up, precision=lax.Precision.HIGHEST, preferred_elem...  3.45 us
  transfers between devices with their start and end apart: 2, of which 1 were waited for; matrix products, arithmetic and copies ran while one was open for 12% of the time, Pallas kernels for 0%

commit v1 on v0

v1 whole, which is shorter than its diff:
```python
import jax
import jax.numpy as jnp
from jax import lax
from jax.experimental import pallas as pl
from jax.experimental.pallas import tpu as pltpu
from jax.sharding import PartitionSpec as P

BLOCK = 16
adapter_scale = 0.25
beta_one = 0.9
beta_two = 0.95

MESH = pl.DeviceIdType.MESH
NZ = 16
NC = 16
F32 = jnp.float32
BF16 = jnp.bfloat16


def split3(lhs, rhs):
    lhs_hi = lhs.astype(BF16)
    lhs_lo = (lhs - lhs_hi.astype(F32)).astype(BF16)
    rhs_hi = rhs.astype(BF16)
    rhs_lo = (rhs - rhs_hi.astype(F32)).astype(BF16)
    dot = lambda a, b: jnp.dot(a, b, preferred_element_type=F32)
    return dot(lhs_hi, rhs_hi) + (dot(lhs_hi, rhs_lo) + dot(lhs_lo, rhs_hi))


def contract_rows(lhs, rhs):
    return lax.dot_general(lhs, rhs, (((0,), (0,)), ((), ())), preferred_element_type=F32)


def kernel(
    tok, og, master, od, ou, fd, fu,
    merged, w, out, g,
    a_all, b_all, og_all, master_v, merged_v, w_v, od_v, ou_v, fd_v, fu_v,
    part, rs, hb_all, gtmp, gsend, grecv, gbuf, acc, stage,
    ld_sem, st_sem, b_send, b_recv, x_recv, y_recv, c_recv, a_send,
    rs_send, rs_recv, hb_send, hb_recv, og_sem, g_send, g_recv, gx_sem, o_send, o_recv,
):
    z = lax.axis_index("row")
    c = lax.axis_index("col")
    h = lax.axis_index("rep")
    other = 1 - h
    y = lax.div(c, 4)
    lo = lax.rem(lax.div(c, 2), 2)
    core = lax.rem(c, 2)
    px = 2 * h + lo
    me = h * NC + c

    def ring(d):
        return (lax.rem(z + (d + NZ), NZ), c, h)

    def plane(j):
        return (z, lax.rem(j, NC), lax.div(j, NC))

    def slot(xr, yr):
        pos = lax.rem(px + xr, 4)
        return lax.div(pos, 2) * NC + lax.rem(y + yr, 4) * 4 + lax.rem(pos, 2) * 2 + core

    def x_dev(xr):
        return plane(slot(xr, 0))

    def y_dev(yr):
        return plane(slot(0, yr))

    partner_core = (z, c + 1 - 2 * core, h)
    partner_rep = (z, c, other)

    def send(src, dst, send_sem, recv_sem, device):
        pltpu.make_async_remote_copy(
            src_ref=src, dst_ref=dst, send_sem=send_sem, recv_sem=recv_sem,
            device_id=device, device_id_type=MESH,
        ).start()

    def arrived(ref, sem):
        pltpu.make_async_remote_copy(
            src_ref=ref, dst_ref=ref, send_sem=a_send, recv_sem=sem,
            device_id=partner_core, device_id_type=MESH,
        ).wait_recv()

    def sent(ref, sem):
        pltpu.make_async_remote_copy(
            src_ref=ref, dst_ref=ref, send_sem=sem, recv_sem=a_send,
            device_id=partner_core, device_id_type=MESH,
        ).wait_send()

    loads = [
        pltpu.make_async_copy(src, dst, ld_sem.at[i])
        for i, (src, dst) in enumerate(
            [(od, od_v), (ou, ou_v), (master, master_v), (tok, a_all.at[me]), (fd, fd_v),
             (og, og_all.at[h]), (fu, fu_v)]
        )
    ]
    for load in loads:
        load.start()
    barrier = pltpu.get_barrier_semaphore()

    def greet_plane(d, carry):
        pl.semaphore_signal(barrier, inc=1, device_id=plane(lax.rem(me + d, 2 * NC)), device_id_type=MESH)
        return carry

    def greet_ring(d, carry):
        pl.semaphore_signal(barrier, inc=1, device_id=ring(d), device_id_type=MESH)
        return carry

    lax.fori_loop(1, 2 * NC, greet_plane, 0)
    lax.fori_loop(1, NZ, greet_ring, 0)

    for load in loads[:3]:
        load.wait()

    def merge(half):
        cols = pl.ds(pl.multiple_of(half * 256, 256), 256)
        both = master_v[:, cols] + adapter_scale * split3(od_v[...], ou_v[:, cols])
        merged_v[:, cols] = both
        w_v[:, cols] = both.astype(BF16)
        return both.astype(BF16)

    b_all[z] = merge(h)

    for load in loads[3:]:
        load.wait()
    down_cast = fd_v[...].astype(BF16)
    up_cast = fu_v[...].astype(BF16)
    hidden = jnp.dot(a_all[me], down_cast, preferred_element_type=F32)
    part[:, :, 0:128] = hidden.reshape(NC, 16, 128)
    backward = lax.dot_general(
        og_all[h], up_cast, (((1,), (1,)), ((), ())), preferred_element_type=F32
    )
    part[:, :, 128:256] = backward.reshape(NC, 16, 128)
    merge(other)
    stores = [
        pltpu.make_async_copy(merged_v, merged, st_sem.at[0]),
        pltpu.make_async_copy(w_v, w, st_sem.at[1]),
    ]
    for store in stores:
        store.start()

    pl.semaphore_wait(barrier, 2 * NC - 1 + NZ - 1)

    def chunk(zz, q):
        return b_all.at[zz, pl.ds((q % 2) * 256, 256), pl.ds((q // 2) * 128, 128)]

    def b_out(direction, step, q):
        sign = 1 if direction == 0 else -1
        origin = ring(-sign * (step - 1))[0]
        send(chunk(origin, q), chunk(origin, q), b_send, b_recv.at[direction, step - 1, q], ring(sign))

    def b_in(direction, step, q):
        sign = 1 if direction == 0 else -1
        origin = ring(-sign * step)[0]
        arrived(chunk(origin, q), b_recv.at[direction, step - 1, q])

    for q in range(4):
        for direction in (0, 1):
            b_out(direction, 1, q)

    def rs_out(d, carry):
        to = lax.rem(c + d, NC)
        send(part.at[to], rs.at[d - 1], rs_send, rs_recv, (z, to, h))
        return carry

    lax.fori_loop(1, NC, rs_out, 0)

    def a_out(at, recv_sem, device):
        send(a_all.at[at], a_all.at[at], a_send, recv_sem, device)

    forward = lax.select(core == 0, 3, 1)
    onward = lax.select(core == 0, 1, 3)

    def x_own():
        a_out(me, x_recv.at[3], x_dev(1))
        a_out(me, x_recv.at[1], x_dev(3))

    def x_in(xr):
        arrived(a_all.at[slot(xr, 0)], x_recv.at[xr])

    def x_forward():
        a_out(slot(forward, 0), x_recv.at[2], x_dev(onward))

    def core_out(xr, yr):
        a_out(slot(xr, yr), c_recv.at[xr], partner_core)

    def y_own(xr):
        a_out(slot(xr, 0), y_recv.at[xr, 3], y_dev(1))
        a_out(slot(xr, 0), y_recv.at[xr, 1], y_dev(3))

    def y_in(xr, yr):
        arrived(a_all.at[slot(xr, yr)], y_recv.at[xr, yr])

    def y_forward(xr):
        a_out(slot(xr, forward), y_recv.at[xr, 2], y_dev(onward))

    x_own()
    y_own(0)
    core_out(0, 0)
    send(og_all.at[h], og_all.at[h], og_sem.at[0], og_sem.at[1], partner_rep)

    def sum_rows():
        arrived(rs, rs_recv)
        total = part[c]
        for d in range(NC - 1):
            total = total + rs[d]
        hb_all[me] = total.astype(BF16)

        def hb_out(d, carry):
            send(hb_all.at[me], hb_all.at[me], hb_send, hb_recv, plane(lax.rem(me + d, 2 * NC)))
            return carry

        lax.fori_loop(1, 2 * NC, hb_out, 0)

    def rows_of(hp):
        return hb_all[pl.ds(hp * NC, NC)].reshape(256, 256)

    def start_outputs():
        arrived(hb_all.at[pl.ds(0, 2 * NC - 1)], hb_recv)
        cols = pl.ds(pl.multiple_of(h * 256, 256), 256)
        up_half = fu_v[:, cols].astype(BF16)
        for hp in (0, 1):
            acc[hp] = adapter_scale * jnp.dot(rows_of(hp)[:, :128], up_half, preferred_element_type=F32)

    def gradients():
        arrived(og_all.at[other], og_sem.at[1])
        down = jnp.zeros((512, 128), F32)
        up = jnp.zeros((512, 128), F32)
        for hp in (0, 1):
            rows = rows_of(hp)
            down = down + contract_rows(a_all[hp * NC + c], rows[:, 128:])
            up = up + contract_rows(og_all[hp], rows[:, :128])
        gtmp[0] = (adapter_scale * down).reshape(NZ, 2, 16, 128)
        gtmp[1] = (adapter_scale * up).reshape(NZ, 2, 16, 128)
        for u in (0, 1):
            gsend[:, u] = gtmp[u, :, h].astype(BF16)

        def g_out(d, carry):
            to = lax.rem(z + d, NZ)
            send(gsend.at[to], grecv.at[d - 1], g_send, g_recv, (to, c, h))
            return carry

        lax.fori_loop(1, NZ, g_out, 0)

    def sum_gradients():
        arrived(grecv, g_recv)
        for u in (0, 1):
            total = gtmp[u, z, h]
            for d in range(NZ - 1):
                total = total + grecv[d, u].astype(F32)
            gbuf[h, u] = total
        send(gbuf.at[h], gbuf.at[h], gx_sem.at[0], gx_sem.at[1], partner_rep)

    def end_gradients():
        arrived(gbuf.at[other], gx_sem.at[1])
        g[...] = gbuf[...]

    def product(zz):
        def one(hp, carry):
            acc[hp] += jnp.dot(a_all[hp * NC + zz], b_all[zz], preferred_element_type=F32)
            return carry

        lax.fori_loop(0, 2, one, 0)

    def products(first, last):
        def one(s, carry):
            product(lax.rem(z + s, NZ))
            product(lax.rem(z + (NZ - s), NZ))
            return carry

        lax.fori_loop(first, last + 1, one, 0)

    def first_products():
        for xr in (0, 3, 1, 2):
            arrived(a_all.at[pl.ds(0, 4)], c_recv.at[xr])
        product(z)
        products(1, 4)

    def x_near():
        for xr in (3, 1):
            x_in(xr)
        x_forward()
        for xr in (3, 1):
            core_out(xr, 0)

    def x_far():
        x_in(2)
        y_own(2)
        core_out(2, 0)

    def y_near(xr):
        y_in(xr, 3)
        y_in(xr, 1)
        y_forward(xr)
        core_out(xr, 3)
        core_out(xr, 1)

    def y_far(xr):
        y_in(xr, 2)
        core_out(xr, 2)

    after = {
        1: [sum_rows],
        3: [x_near, lambda: (y_own(3), y_own(1))],
        5: [start_outputs, lambda: y_near(0)],
        6: [x_far],
        7: [gradients],
        9: [lambda: y_far(0)],
        13: [lambda: y_near(3)],
        15: [lambda: y_near(1)],
        16: [sum_gradients],
        17: [lambda: y_far(3)],
        18: [lambda: y_near(2)],
        20: [lambda: y_far(1), end_gradients],
        22: [lambda: y_far(2)],
        23: [first_products],
        24: [lambda: products(5, 5)],
        25: [lambda: products(6, 6)],
        27: [lambda: products(7, 7)],
    }
    for tick in range(28):
        step, q = tick // 4 + 1, tick % 4
        for direction in (0, 1):
            b_in(direction, step, q)
            if step < 7 or q % 2 == direction:
                b_out(direction, step + 1, q)
        for action in after.get(tick, ()):
            action()

    far = lax.rem(z + 8, NZ)
    outs = []
    for part_of in (0, 1):
        for direction in (0, 1):
            b_in(direction, 8, 2 * part_of + direction)
        cols = pl.ds(part_of * 128, 128)
        there = pl.ds(pl.multiple_of(h * 256 + part_of * 128, 128), 128)
        for hp in (other, h):
            total = acc[hp, :, cols] + jnp.dot(
                a_all[hp * NC + far], b_all[far, :, cols], preferred_element_type=F32
            )
            stage[hp, part_of] = total.astype(BF16)
            if hp is other:
                send(stage.at[other, part_of], out.at[:, there], o_send.at[part_of], o_recv.at[part_of], partner_rep)
            else:
                keep = pltpu.make_async_copy(stage.at[h, part_of], out.at[:, there], st_sem.at[2 + part_of])
                keep.start()
                stores.append(keep)

    for store in stores:
        store.wait()
    sent(a_all.at[pl.ds(0, 31)], a_send)
    sent(b_all.at[pl.ds(0, 15)], b_send)
    sent(rs, rs_send)
    sent(hb_all.at[pl.ds(0, 2 * NC - 1)], hb_send)
    sent(og_all.at[h], og_sem.at[0])
    sent(grecv, g_send)
    sent(gbuf.at[h], gx_sem.at[0])
    for part_of in (0, 1):
        sent(stage.at[other, part_of], o_send.at[part_of])
        there = pl.ds(pl.multiple_of(other * 256 + part_of * 128, 128), 128)
        arrived(out.at[:, there], o_recv.at[part_of])


def adam_moments(first_moment, second_moment, keep_scale, gradient):
    first_new = beta_one * keep_scale * first_moment + (1.0 - beta_one) * gradient
    second_new = beta_two * keep_scale * second_moment + (1.0 - beta_two) * gradient * gradient
    return (first_new, second_new)


def body(
    tokens, output_gradient, master_weight, old_down, old_up, fresh_down, fresh_up,
    m_down, v_down, m_up, v_up, keep_down, keep_up,
):
    dma = pltpu.SemaphoreType.DMA
    vmem = pltpu.VMEM
    merged_weight, w_copy, outputs, g = pl.pallas_call(
        kernel,
        out_shape=(
            jax.ShapeDtypeStruct((512, 512), F32),
            jax.ShapeDtypeStruct((512, 512), BF16),
            jax.ShapeDtypeStruct((256, 512), BF16),
            jax.ShapeDtypeStruct((2, 2, 16, 128), F32),
        ),
        in_specs=[pl.BlockSpec(memory_space=pl.ANY)] * 7,
        out_specs=(
            pl.BlockSpec(memory_space=pl.ANY),
            pl.BlockSpec(memory_space=pl.ANY),
            pl.BlockSpec(memory_space=pl.ANY),
            pl.BlockSpec(memory_space=pltpu.VMEM),
        ),
        scratch_shapes=[
            vmem((2 * NC, 256, 512), BF16),
            vmem((NZ, 512, 256), BF16),
            vmem((2, 256, 512), BF16),
            vmem((512, 512), F32),
            vmem((512, 512), F32),
            vmem((512, 512), BF16),
            vmem((512, 128), F32),
            vmem((128, 512), F32),
            vmem((512, 128), F32),
            vmem((128, 512), F32),
            vmem((NC, 16, 256), F32),
            vmem((NC - 1, 16, 256), F32),
            vmem((2 * NC, 16, 256), BF16),
            vmem((2, NZ, 2, 16, 128), F32),
            vmem((NZ, 2, 16, 128), BF16),
            vmem((NZ - 1, 2, 16, 128), BF16),
            vmem((2, 2, 16, 128), F32),
            vmem((2, 256, 256), F32),
            vmem((2, 2, 256, 128), BF16),
            dma((7,)),
            dma((4,)),
            dma,
            dma((2, 8, 4)),
            dma((4,)),
            dma((4, 4)),
            dma((4,)),
            dma,
            dma,
            dma,
            dma,
            dma,
            dma((2,)),
            dma,
            dma,
            dma((2,)),
            dma((2,)),
            dma((2,)),
        ],
        compiler_params=pltpu.CompilerParams(
            collective_id=0, has_side_effects=True, vmem_limit_bytes=48 * 1024 * 1024
        ),
        name="relora_step",
    )(tokens, output_gradient, master_weight, old_down, old_up, fresh_down, fresh_up)
    down_rows = g[:, 0].reshape(32, 128)
    up_rows = g[:, 1].reshape(32, 128)
    keep_rows = jnp.repeat(keep_down.astype(F32), BLOCK)[:, None]
    keep_cols = jnp.repeat(keep_up.astype(F32), BLOCK)[None, :]
    m_down_new, v_down_new = adam_moments(m_down, v_down, keep_rows, down_rows)
    m_up_new, v_up_new = adam_moments(m_up, v_up, keep_cols, up_rows.T)
    return (merged_weight, w_copy, outputs, m_down_new, v_down_new, m_up_new, v_up_new)


def solution(mesh):
    both = P(("row", "rep"), "col")
    tile = P("row", "col")
    down = P(("col", "row"), None)
    up = P(None, ("col", "row"))
    flags = P(("col", "row"))
    return jax.shard_map(
        body,
        mesh=mesh,
        in_specs=(
            both, both, tile, P("row", None), P(None, "col"), P("col", None), P(None, "col"),
            down, down, up, up, flags, flags,
        ),
        out_specs=(tile, tile, both, down, down, up, up),
        check_vma=False,
    )
```

time: 154 us -> 95.7 us (0.62)
  blocking collectives: 85.7 us -> 0 us
  Pallas kernels: 0 us -> 82 us
  waiting for transfers between devices: 18.5 us -> 0 us
  between operations: 14.4 us -> 0.71 us
  matrix products: 12.6 us -> 0 us
  local copies, waits for them, and re-layouts: 15.3 us -> 11.1 us
  starting transfers between devices: 3.64 us -> 0 us
  other arithmetic: 3.04 us -> 1.38 us
    all_to_all x6 -> x0, blocking collectives: 85.7 us -> none  [the longest x4 38 us: copy_for_each(): lax.all_to_all(jnp.broadcast_to(shard[None], (length, *shard.shape)), axi...]
    pallas_call x0 -> x1, Pallas kernels: none -> 82 us  [body(): pl.pallas_call(kernel, out_shape=(jax.ShapeDtypeStruct((512, 512), F32),...]
    all_to_all x1 -> x0, waiting for transfers between devices: 18.5 us -> none  [copy_for_each(): lax.all_to_all(jnp.broadcast_to(shard[None], (length, *shard.shape)), axi...]
    dot_general x7 -> x0, matrix products: 12.6 us -> none  [the longest x1 6.98 us: body(): jnp.dot(gathered, lax.all_gather(w_copy, 'row', axis=0, tiled=True), pref...]
    unnamed x25 -> x29, local copies, waits for them, and re-layouts: 2.13 us -> 10.4 us
    transpose x1 -> x0, local copies, waits for them, and re-layouts: 6.36 us -> none  [in_order(): return jnp.moveaxis(tiles, 0, dim).reshape(dims)]
    all_to_all x1 -> x0, starting transfers between devices: 3.6 us -> none  [copy_for_each(): lax.all_to_all(jnp.broadcast_to(shard[None], (length, *shard.shape)), axi...]
    broadcast_in_dim x10 -> x4, local copies, waits for them, and re-layouts: 3 us -> 0.28 us  [the longest x2 0.14 us: body(): keep_rows = jnp.repeat(keep_down.astype(F32), BLOCK)[:, None]]
  transfers between devices with their start and end apart: 2 -> 0, of which waited for: 1 -> 0; matrix products, arithmetic and copies ran while one was open for 12% -> 0% of each run, Pallas kernels for 0% -> 0%
where the time goes in v1:
time: 95.7 us; the launch traced here: 95.2 us
  Pallas kernels  82 us (86%)
  local copies, waits for them, and re-layouts  11.1 us (12%)
  other arithmetic  1.38 us (1%)
    pallas_call x1, Pallas kernels, body(): pl.pallas_call(kernel, out_shape=(jax.ShapeDtypeStruct((512, 512), F32),...  82 us
    unnamed x29, local copies, waits for them, and re-layouts  10.4 us

profile of v1, /device:TPU:1, one launch (start us, length us, event | category | flops | bytes accessed | tf_op | source)
XLA Modules:
  0.0 95.2 jit_solution(5616185223488522917)
XLA Ops:
  0.6 0.0 copy-start
  0.6 1.2 %copy-done = f32[512,512]{1,0:T(8,128)S(1)} copy-done((f32[512,512]{1,0:T(8,128)S(1)}, f32[512,512]{1,0:T(8,128)}, u32[]{:S(2)}) %copy-start) | copy-done | bytes 1048600
  1.9 0.0 copy-start.1
  1.9 0.9 copy-done.1
  2.8 0.9 copy-done.2
  3.8 0.9 copy-done.3
  4.7 0.9 copy-done.4
  5.7 0.9 copy-done.5
  6.6 0.9 copy-done.6
  7.6 82.0 %relora_step.1 = (f32[512,512]{1,0:T(8,128)S(1)}, bf16[512,512]{1,0:T(8,128)(2,1)S(1)}, bf16[256,512]{1,0:T(8,128)(2,1)S(1)}, f32[2,2,16,128]{3,2,1,0:T(8,128)S(1)}) custom-call(bf16[256,512]{1,0:T(8,128)(2,1)S(1)} %copy-done.1, bf16[256,512]{1,0:T(8,128)(2,1)S(1)} %copy-done.2, f32[512,512]{1,0:T(8,128)S(1)} %copy-done, f32[512,128]{1,0:T(8,128)S(1)} %copy-done.3, ...), custom_call_target="tpu_custom_call" | custom-call | tf_op jit(solution)/shard_map/relora_step/pallas_call | solution.py:374
  89.6 0.0 copy-start.7
  89.6 0.0 copy-start.8
  89.6 0.0 copy-start.11
  89.7 0.6 copy-done.11
  90.3 0.1 broadcast_in_dim.11
  90.4 0.1 mul.127
  90.5 0.1 broadcast_in_dim.10
  90.5 0.1 mul.120
  90.6 0.0 copy-done.7
  90.6 0.0 copy-done.8
  90.6 0.7 fusion
  91.3 0.0 copy-done.12
  91.3 0.1 broadcast_in_dim.13
  91.4 0.1 mul.140
  91.5 0.1 broadcast_in_dim.12
  91.6 0.1 mul.134
  91.6 0.0 copy-done.10
  91.7 0.4 copy-done.9
  92.0 0.7 fusion.1
  92.7 1.0 %copy.23 = f32[512,512]{1,0:T(8,128)} copy(f32[512,512]{1,0:T(8,128)S(1)} %get-tuple-element.32) | data formatting | bytes 2097152
  93.7 0.8 copy.24
  94.5 0.7 copy.25
  (11 shorter events, 0.0 us)
Async XLA Ops:
  0.6 1.2 %copy-start = (f32[512,512]{1,0:T(8,128)S(1)}, f32[512,512]{1,0:T(8,128)}, u32[]{:S(2)}) copy-start(f32[512,512]{1,0:T(8,128)} %master.1) | copy-start | bytes 3145732
  1.9 0.9 copy-start.1
  2.8 0.9 copy-start.2
  3.8 0.9 copy-start.3
  4.7 0.9 copy-start.4
  5.7 0.9 copy-start.5
  6.6 0.9 copy-start.6
  89.6 1.0 %copy-start.7 = (f32[32,128]{1,0:T(8,128)S(1)}, f32[32,128]{1,0:T(8,128)}, u32[]{:S(2)}) copy-start(f32[32,128]{1,0:T(8,128)} %param.21) | copy-start | bytes 49156
  89.6 1.0 %copy-start.8 = (f32[32,128]{1,0:T(8,128)S(1)}, f32[32,128]{1,0:T(8,128)}, u32[]{:S(2)}) copy-start(f32[32,128]{1,0:T(8,128)} %param.20) | copy-start | bytes 49156
  89.6 0.7 copy-start.11
  90.6 0.7 copy-start.12
  90.6 1.0 %copy-start.10 = (f32[128,32]{0,1:T(8,128)S(1)}, f32[128,32]{0,1:T(8,128)}, u32[]{:S(2)}) copy-start(f32[128,32]{0,1:T(8,128)} %param.22) | copy-start | bytes 49156
  91.3 0.7 copy-start.9

commit v2 on v1

--- a/solution.py
+++ b/solution.py
@@ -31,12 +31,12 @@
 
 
 def kernel(
-    tok, og, master, od, ou, fd, fu,
-    merged, w, out, g,
-    a_all, b_all, og_all, master_v, merged_v, w_v, od_v, ou_v, fd_v, fu_v,
-    part, rs, hb_all, gtmp, gsend, grecv, gbuf, acc, stage,
-    ld_sem, st_sem, b_send, b_recv, x_recv, y_recv, c_recv, a_send,
-    rs_send, rs_recv, hb_send, hb_recv, og_sem, g_send, g_recv, gx_sem, o_send, o_recv,
+    tok, og, master, od, ou, fd, fu, md, vd, mu, vu, kd, ku,
+    merged, w, out, moments,
+    a_all, b_all, og_v, master_v, merged_v, w_v, moments_v, od_v, ou_v, fd_v, fu_v,
+    part, rs, hb_all, gtmp, up_send, up_recv, gsum, gsend, grecv, gbuf, acc, stage, old_moments, flags,
+    ld_sem, st_sem, b_send, b_recv, p1_recv, p2_recv, c_recv, a_send,
+    rs_send, rs_recv, hb_send, hb_recv, up_sem, g_send, g_recv, gx_sem, o_send, o_recv, far_sem,
 ):
     z = lax.axis_index("row")
     c = lax.axis_index("col")
@@ -89,7 +89,8 @@
         pltpu.make_async_copy(src, dst, ld_sem.at[i])
         for i, (src, dst) in enumerate(
             [(od, od_v), (ou, ou_v), (master, master_v), (tok, a_all.at[me]), (fd, fd_v),
-             (og, og_all.at[h]), (fu, fu_v)]
+             (og, og_v), (fu, fu_v), (md, old_moments.at[0]), (vd, old_moments.at[1]),
+             (mu, old_moments.at[2]), (vu, old_moments.at[3]), (kd, flags.at[0]), (ku, flags.at[1])]
         )
     ]
     for load in loads:
@@ -105,7 +106,8 @@
         return carry
 
     lax.fori_loop(1, 2 * NC, greet_plane, 0)
-    lax.fori_loop(1, NZ, greet_ring, 0)
+    greet_ring(1, 0)
+    greet_ring(-1, 0)
 
     for load in loads[:3]:
         load.wait()
@@ -119,25 +121,34 @@
 
     b_all[z] = merge(h)
 
-    for load in loads[3:]:
+    for load in loads[3:7]:
         load.wait()
     down_cast = fd_v[...].astype(BF16)
     up_cast = fu_v[...].astype(BF16)
     hidden = jnp.dot(a_all[me], down_cast, preferred_element_type=F32)
     part[:, :, 0:128] = hidden.reshape(NC, 16, 128)
     backward = lax.dot_general(
-        og_all[h], up_cast, (((1,), (1,)), ((), ())), preferred_element_type=F32
+        og_v[...], up_cast, (((1,), (1,)), ((), ())), preferred_element_type=F32
     )
     part[:, :, 128:256] = backward.reshape(NC, 16, 128)
     merge(other)
     stores = [
-        pltpu.make_async_copy(merged_v, merged, st_sem.at[0]),
-        pltpu.make_async_copy(w_v, w, st_sem.at[1]),
+        pltpu.make_async_copy(merged_v, merged, st_sem.at[2]),
+        pltpu.make_async_copy(w_v, w, st_sem.at[3]),
     ]
     for store in stores:
         store.start()
 
-    pl.semaphore_wait(barrier, 2 * NC - 1 + NZ - 1)
+    pl.semaphore_wait(barrier, 2 * NC - 1 + 2)
+
+    def tell(i, distance):
+        for d in (distance, -distance):
+            pl.semaphore_signal(far_sem.at[i], inc=1, device_id=ring(d), device_id_type=MESH)
+
+    def told(i):
+        pl.semaphore_wait(far_sem.at[i], 2)
+
+    tell(0, 1)
 
     def chunk(zz, q):
         return b_all.at[zz, pl.ds((q % 2) * 256, 256), pl.ds((q // 2) * 128, 128)]
@@ -163,39 +174,59 @@
 
     lax.fori_loop(1, NC, rs_out, 0)
 
-    def a_out(at, recv_sem, device):
-        send(a_all.at[at], a_all.at[at], a_send, recv_sem, device)
-
     forward = lax.select(core == 0, 3, 1)
     onward = lax.select(core == 0, 1, 3)
 
-    def x_own():
-        a_out(me, x_recv.at[3], x_dev(1))
-        a_out(me, x_recv.at[1], x_dev(3))
-
-    def x_in(xr):
-        arrived(a_all.at[slot(xr, 0)], x_recv.at[xr])
-
-    def x_forward():
-        a_out(slot(forward, 0), x_recv.at[2], x_dev(onward))
-
-    def core_out(xr, yr):
-        a_out(slot(xr, yr), c_recv.at[xr], partner_core)
-
-    def y_own(xr):
-        a_out(slot(xr, 0), y_recv.at[xr, 3], y_dev(1))
-        a_out(slot(xr, 0), y_recv.at[xr, 1], y_dev(3))
-
-    def y_in(xr, yr):
-        arrived(a_all.at[slot(xr, yr)], y_recv.at[xr, yr])
-
-    def y_forward(xr):
-        a_out(slot(xr, forward), y_recv.at[xr, 2], y_dev(onward))
-
-    x_own()
-    y_own(0)
-    core_out(0, 0)
-    send(og_all.at[h], og_all.at[h], og_sem.at[0], og_sem.at[1], partner_rep)
+    def at(half, r1, r2):
+        return a_all.at[slot(r1, r2) if half == 0 else slot(r2, r1), pl.ds(half * 128, 128)]
+
+    def along(axis, r):
+        return x_dev(r) if axis == 0 else y_dev(r)
+
+    def a_out(ref, recv_sem, device):
+        send(ref, ref, a_send, recv_sem, device)
+
+    def core_out(half, r1, r2):
+        a_out(at(half, r1, r2), c_recv.at[half, r1], partner_core)
+
+    def p1_own(half):
+        for d in (1, 3):
+            a_out(at(half, 0, 0), p1_recv.at[half, 4 - d], along(half, d))
+
+    def p2_own(half, r1):
+        for d in (1, 3):
+            a_out(at(half, r1, 0), p2_recv.at[half, r1, 4 - d], along(1 - half, d))
+        core_out(half, r1, 0)
+
+    def p1_near():
+        for half in (0, 1):
+            for r in (3, 1):
+                arrived(at(half, r, 0), p1_recv.at[half, r])
+            a_out(at(half, forward, 0), p1_recv.at[half, 2], along(half, onward))
+        for half in (0, 1):
+            p2_own(half, 3)
+            p2_own(half, 1)
+
+    def p1_far():
+        for half in (0, 1):
+            arrived(at(half, 2, 0), p1_recv.at[half, 2])
+            p2_own(half, 2)
+
+    def p2_near(half, r1):
+        for r in (3, 1):
+            arrived(at(half, r1, r), p2_recv.at[half, r1, r])
+        a_out(at(half, r1, forward), p2_recv.at[half, r1, 2], along(1 - half, onward))
+        core_out(half, r1, 3)
+        core_out(half, r1, 1)
+
+    def p2_far(half, r1):
+        arrived(at(half, r1, 2), p2_recv.at[half, r1, 2])
+        core_out(half, r1, 2)
+
+    for half in (0, 1):
+        p1_own(half)
+    for half in (0, 1):
+        p2_own(half, 0)
 
     def sum_rows():
         arrived(rs, rs_recv)
@@ -220,18 +251,24 @@
         for hp in (0, 1):
             acc[hp] = adapter_scale * jnp.dot(rows_of(hp)[:, :128], up_half, preferred_element_type=F32)
 
+    def up_gradient():
+        up = contract_rows(og_v[...], hb_all[pl.ds(h * NC, NC)].reshape(256, 256)[:, :128])
+        gtmp[...] = (adapter_scale * up).reshape(NZ, 2, 16, 128)
+        up_send[...] = gtmp[:, other].astype(BF16)
+        gsum[1] = gtmp[:, h]
+        send(up_send, up_recv, up_sem.at[0], up_sem.at[1], partner_rep)
+
     def gradients():
-        arrived(og_all.at[other], og_sem.at[1])
         down = jnp.zeros((512, 128), F32)
-        up = jnp.zeros((512, 128), F32)
         for hp in (0, 1):
-            rows = rows_of(hp)
-            down = down + contract_rows(a_all[hp * NC + c], rows[:, 128:])
-            up = up + contract_rows(og_all[hp], rows[:, :128])
-        gtmp[0] = (adapter_scale * down).reshape(NZ, 2, 16, 128)
-        gtmp[1] = (adapter_scale * up).reshape(NZ, 2, 16, 128)
+            down = down + contract_rows(a_all[hp * NC + c], rows_of(hp)[:, 128:])
+        gtmp[...] = (adapter_scale * down).reshape(NZ, 2, 16, 128)
+        gsum[0] = gtmp[:, h]
+        arrived(up_recv, up_sem.at[1])
+        gsum[1] += up_recv[...].astype(F32)
         for u in (0, 1):
-            gsend[:, u] = gtmp[u, :, h].astype(BF16)
+            gsend[:, u] = gsum[u].astype(BF16)
+        told(2)
 
         def g_out(d, carry):
             to = lax.rem(z + d, NZ)
@@ -243,7 +280,7 @@
     def sum_gradients():
         arrived(grecv, g_recv)
         for u in (0, 1):
-            total = gtmp[u, z, h]
+            total = gsum[u, z]
             for d in range(NZ - 1):
                 total = total + grecv[d, u].astype(F32)
             gbuf[h, u] = total
@@ -251,7 +288,20 @@
 
     def end_gradients():
         arrived(gbuf.at[other], gx_sem.at[1])
-        g[...] = gbuf[...]
+        for load in loads[7:]:
+            load.wait()
+        for u in (0, 1):
+            for hp in (0, 1):
+                rows = pl.ds(hp * 16, 16)
+                keep = flags[u, hp].astype(F32)
+                gradient = gbuf[hp, u]
+                moments_v[2 * u, rows, :] = (beta_one * keep) * old_moments[2 * u, rows, :] + (1.0 - beta_one) * gradient
+                moments_v[2 * u + 1, rows, :] = (beta_two * keep) * old_moments[2 * u + 1, rows, :] + (
+                    (1.0 - beta_two) * gradient * gradient
+                )
+        store = pltpu.make_async_copy(moments_v, moments, st_sem.at[4])
+        store.start()
+        stores.append(store)
 
     def product(zz):
         def one(hp, carry):
@@ -269,51 +319,41 @@
         lax.fori_loop(first, last + 1, one, 0)
 
     def first_products():
-        for xr in (0, 3, 1, 2):
-            arrived(a_all.at[pl.ds(0, 4)], c_recv.at[xr])
+        for half in (0, 1):
+            for r1 in range(4):
+                arrived(a_all.at[pl.ds(0, 2)], c_recv.at[half, r1])
         product(z)
-        products(1, 4)
-
-    def x_near():
-        for xr in (3, 1):
-            x_in(xr)
-        x_forward()
-        for xr in (3, 1):
-            core_out(xr, 0)
-
-    def x_far():
-        x_in(2)
-        y_own(2)
-        core_out(2, 0)
-
-    def y_near(xr):
-        y_in(xr, 3)
-        y_in(xr, 1)
-        y_forward(xr)
-        core_out(xr, 3)
-        core_out(xr, 1)
-
-    def y_far(xr):
-        y_in(xr, 2)
-        core_out(xr, 2)
+        products(1, 1)
+
+    def doubling():
+        told(0)
+        tell(1, 2)
+
+    def doubled():
+        told(1)
+        tell(2, 4)
 
     after = {
+        0: [doubling],
         1: [sum_rows],
-        3: [x_near, lambda: (y_own(3), y_own(1))],
-        5: [start_outputs, lambda: y_near(0)],
-        6: [x_far],
-        7: [gradients],
-        9: [lambda: y_far(0)],
-        13: [lambda: y_near(3)],
-        15: [lambda: y_near(1)],
-        16: [sum_gradients],
-        17: [lambda: y_far(3)],
-        18: [lambda: y_near(2)],
-        20: [lambda: y_far(1), end_gradients],
-        22: [lambda: y_far(2)],
-        23: [first_products],
-        24: [lambda: products(5, 5)],
-        25: [lambda: products(6, 6)],
+        2: [doubled],
+        3: [p1_near],
+        5: [p1_far, start_outputs, up_gradient],
+        6: [lambda: p2_near(1, 0), lambda: p2_near(0, 0)],
+        8: [lambda: p2_far(1, 0), lambda: p2_far(0, 0), gradients],
+        10: [lambda: p2_near(0, 3), lambda: p2_near(1, 3)],
+        11: [lambda: p2_near(0, 1), lambda: p2_near(1, 1)],
+        12: [lambda: p2_near(0, 2), lambda: p2_near(1, 2)],
+        14: [lambda: p2_far(0, 3), lambda: p2_far(1, 3)],
+        15: [lambda: p2_far(0, 1), lambda: p2_far(1, 1)],
+        16: [lambda: p2_far(0, 2), lambda: p2_far(1, 2)],
+        17: [sum_gradients],
+        19: [first_products],
+        20: [lambda: products(2, 2), end_gradients],
+        21: [lambda: products(3, 3)],
+        22: [lambda: products(4, 4)],
+        23: [lambda: products(5, 5)],
+        24: [lambda: products(6, 6)],
         27: [lambda: products(7, 7)],
     }
     for tick in range(28):
@@ -340,7 +380,7 @@
             if hp is other:
                 send(stage.at[other, part_of], out.at[:, there], o_send.at[part_of], o_recv.at[part_of], partner_rep)
             else:
-                keep = pltpu.make_async_copy(stage.at[h, part_of], out.at[:, there], st_sem.at[2 + part_of])
+                keep = pltpu.make_async_copy(stage.at[h, part_of], out.at[:, there], st_sem.at[part_of])
                 keep.start()
                 stores.append(keep)
 
@@ -350,7 +390,7 @@
     sent(b_all.at[pl.ds(0, 15)], b_send)
     sent(rs, rs_send)
     sent(hb_all.at[pl.ds(0, 2 * NC - 1)], hb_send)
-    sent(og_all.at[h], og_sem.at[0])
+    sent(up_send, up_sem.at[0])
     sent(grecv, g_send)
     sent(gbuf.at[h], gx_sem.at[0])
     for part_of in (0, 1):
@@ -359,10 +399,24 @@
         arrived(out.at[:, there], o_recv.at[part_of])
 
 
-def adam_moments(first_moment, second_moment, keep_scale, gradient):
-    first_new = beta_one * keep_scale * first_moment + (1.0 - beta_one) * gradient
-    second_new = beta_two * keep_scale * second_moment + (1.0 - beta_two) * gradient * gradient
-    return (first_new, second_new)
+def write_out(merged, w, out, moments, merged_to, w_to, out_to, md, vd, mu, vu, merged_v, w_v, out_v, moments_v, sem):
+    loads, stores = [], []
+    for src, mid, dst in ((merged, merged_v, merged_to), (w, w_v, w_to), (out, out_v, out_to)):
+        half = src.shape[0] // 2
+        for rows in (pl.ds(0, half), pl.ds(half, half)):
+            loads.append(pltpu.make_async_copy(src.at[rows], mid.at[rows], sem.at[len(loads)]))
+            stores.append([pltpu.make_async_copy(mid.at[rows], dst.at[rows], sem.at[7 + len(stores)])])
+    loads.append(pltpu.make_async_copy(moments, moments_v, sem.at[6]))
+    stores.append([pltpu.make_async_copy(moments_v.at[i], ref, sem.at[13 + i]) for i, ref in enumerate((md, vd, mu, vu))])
+    for load in loads:
+        load.start()
+    for load, after in zip(loads, stores):
+        load.wait()
+        for store in after:
+            store.start()
+    for after in stores:
+        for store in after:
+            store.wait()
 
 
 def body(
@@ -371,28 +425,25 @@
 ):
     dma = pltpu.SemaphoreType.DMA
     vmem = pltpu.VMEM
-    merged_weight, w_copy, outputs, g = pl.pallas_call(
+    hbm = pl.BlockSpec(memory_space=pltpu.HBM)
+    results = pl.pallas_call(
         kernel,
         out_shape=(
             jax.ShapeDtypeStruct((512, 512), F32),
             jax.ShapeDtypeStruct((512, 512), BF16),
             jax.ShapeDtypeStruct((256, 512), BF16),
-            jax.ShapeDtypeStruct((2, 2, 16, 128), F32),
+            jax.ShapeDtypeStruct((4, 32, 128), F32),
         ),
-        in_specs=[pl.BlockSpec(memory_space=pl.ANY)] * 7,
-        out_specs=(
-            pl.BlockSpec(memory_space=pl.ANY),
-            pl.BlockSpec(memory_space=pl.ANY),
-            pl.BlockSpec(memory_space=pl.ANY),
-            pl.BlockSpec(memory_space=pltpu.VMEM),
-        ),
+        in_specs=[hbm] * 13,
+        out_specs=(hbm,) * 4,
         scratch_shapes=[
             vmem((2 * NC, 256, 512), BF16),
             vmem((NZ, 512, 256), BF16),
-            vmem((2, 256, 512), BF16),
+            vmem((256, 512), BF16),
             vmem((512, 512), F32),
             vmem((512, 512), F32),
             vmem((512, 512), BF16),
+            vmem((4, 32, 128), F32),
             vmem((512, 128), F32),
             vmem((128, 512), F32),
             vmem((512, 128), F32),
@@ -400,19 +451,24 @@
             vmem((NC, 16, 256), F32),
             vmem((NC - 1, 16, 256), F32),
             vmem((2 * NC, 16, 256), BF16),
-            vmem((2, NZ, 2, 16, 128), F32),
+            vmem((NZ, 2, 16, 128), F32),
+            vmem((NZ, 16, 128), BF16),
+            vmem((NZ, 16, 128), BF16),
+            vmem((2, NZ, 16, 128), F32),
             vmem((NZ, 2, 16, 128), BF16),
             vmem((NZ - 1, 2, 16, 128), BF16),
             vmem((2, 2, 16, 128), F32),
             vmem((2, 256, 256), F32),
             vmem((2, 2, 256, 128), BF16),
-            dma((7,)),
-            dma((4,)),
+            vmem((4, 32, 128), F32),
+            pltpu.SMEM((2, 2), jnp.int32),
+            dma((13,)),
+            dma((5,)),
             dma,
             dma((2, 8, 4)),
-            dma((4,)),
-            dma((4, 4)),
-            dma((4,)),
+            dma((2, 4)),
+            dma((2, 4, 4)),
+            dma((2, 4)),
             dma,
             dma,
             dma,
@@ -424,19 +480,34 @@
             dma((2,)),
             dma((2,)),
             dma((2,)),
+            pltpu.SemaphoreType.REGULAR((3,)),
         ],
         compiler_params=pltpu.CompilerParams(
-            collective_id=0, has_side_effects=True, vmem_limit_bytes=48 * 1024 * 1024
+            collective_id=0, has_side_effects=True, vmem_limit_bytes=60 * 1024 * 1024
         ),
         name="relora_step",
-    )(tokens, output_gradient, master_weight, old_down, old_up, fresh_down, fresh_up)
-    down_rows = g[:, 0].reshape(32, 128)
-    up_rows = g[:, 1].reshape(32, 128)
-    keep_rows = jnp.repeat(keep_down.astype(F32), BLOCK)[:, None]
-    keep_cols = jnp.repeat(keep_up.astype(F32), BLOCK)[None, :]
-    m_down_new, v_down_new = adam_moments(m_down, v_down, keep_rows, down_rows)
-    m_up_new, v_up_new = adam_moments(m_up, v_up, keep_cols, up_rows.T)
-    return (merged_weight, w_copy, outputs, m_down_new, v_down_new, m_up_new, v_up_new)
+    )(
+        tokens, output_gradient, master_weight, old_down, old_up, fresh_down, fresh_up,
+        m_down, v_down, m_up.T, v_up.T, keep_down, keep_up,
+    )
+    small = jax.ShapeDtypeStruct((32, 128), F32)
+    merged_weight, w_copy, outputs, md, vd, mu, vu = pl.pallas_call(
+        write_out,
+        out_shape=(
+            jax.ShapeDtypeStruct((512, 512), F32),
+            jax.ShapeDtypeStruct((512, 512), BF16),
+            jax.ShapeDtypeStruct((256, 512), BF16),
+            small, small, small, small,
+        ),
+        in_specs=[hbm] * 4,
+        out_specs=(hbm,) * 7,
+        scratch_shapes=[
+            vmem((512, 512), F32), vmem((512, 512), BF16), vmem((256, 512), BF16), vmem((4, 32, 128), F32), dma((17,)),
+        ],
+        compiler_params=pltpu.CompilerParams(vmem_limit_bytes=60 * 1024 * 1024),
+        name="write_out",
+    )(*results)
+    return (merged_weight, w_copy, outputs, md, vd, mu.T, vu.T)
 
 
 def solution(mesh):

time: 95.7 us -> 82.6 us (0.86)
  local copies, waits for them, and re-layouts: 11.1 us -> 0 us
  other arithmetic: 1.38 us -> 0 us
    unnamed x29 -> x0, local copies, waits for them, and re-layouts: 10.4 us -> none
    pallas_call x1, Pallas kernels: 82 us -> 79.4 us  [body(): pl.pallas_call(kernel, out_shape=(jax.ShapeDtypeStruct((512, 512), F32),...]
    pallas_call x0 -> x1, Pallas kernels: none -> 2.42 us  [body(): pl.pallas_call(write_out, out_shape=(jax.ShapeDtypeStruct((512, 512), F32...]
    add x2 -> x0, other arithmetic: 1.38 us -> none  [adam_moments(): beta_two * keep_scale * second_moment]
where the time goes in v2:
time: 82.6 us; the launch traced here: 82.5 us
  Pallas kernels  81.8 us (99%)
    pallas_call x1, Pallas kernels, body(): pl.pallas_call(kernel, out_shape=(jax.ShapeDtypeStruct((512, 512), F32),...  79.4 us
    pallas_call x1, Pallas kernels, body(): pl.pallas_call(write_out, out_shape=(jax.ShapeDtypeStruct((512, 512), F32...  2.42 us

profile of v2, /device:TPU:1, one launch (start us, length us, event | category | flops | bytes accessed | tf_op | source)
XLA Modules:
  0.0 82.5 jit_solution(6576149648605291900)
XLA Ops:
  0.6 79.4 %relora_step.1 = (f32[512,512]{1,0:T(8,128)}, bf16[512,512]{1,0:T(8,128)(2,1)}, bf16[256,512]{1,0:T(8,128)(2,1)}, f32[4,32,128]{2,1,0:T(8,128)}) custom-call(bf16[256,512]{1,0:T(8,128)(2,1)} %tok.1, bf16[256,512]{1,0:T(8,128)(2,1)} %og.1, f32[512,512]{1,0:T(8,128)} %master.1, f32[512,128]{1,0:T(8,128)} %od.1, f32[128,512]{1,0:T(8,128)} %ou.1, ...), custom_call_target="tpu_custom_call" | custom-call | tf_op jit(solution)/shard_map/relora_step/pallas_call | solution.py:429
  80.0 2.4 %write_out.1 = (f32[512,512]{1,0:T(8,128)}, bf16[512,512]{1,0:T(8,128)(2,1)}, bf16[256,512]{1,0:T(8,128)(2,1)}, f32[32,128]{1,0:T(8,128)}, f32[32,128]{1,0:T(8,1...) custom-call(f32[512,512]{1,0:T(8,128)} %get-tuple-element.18.merged, bf16[512,512]{1,0:T(8,128)(2,1)} %get-tuple-element.19.w, ...), custom_call_target="tpu_custom_call" | custom-call | tf_op jit(solution)/shard_map/write_out/pallas_call | solution.py:494

commit v3 on v2

--- a/solution.py
+++ b/solution.py
@@ -85,41 +85,68 @@
             device_id=partner_core, device_id_type=MESH,
         ).wait_send()
 
+    def columns(half):
+        return pl.ds(pl.multiple_of(half * 256, 256), 256)
+
     loads = [
         pltpu.make_async_copy(src, dst, ld_sem.at[i])
         for i, (src, dst) in enumerate(
-            [(od, od_v), (ou, ou_v), (master, master_v), (tok, a_all.at[me]), (fd, fd_v),
-             (og, og_v), (fu, fu_v), (md, old_moments.at[0]), (vd, old_moments.at[1]),
-             (mu, old_moments.at[2]), (vu, old_moments.at[3]), (kd, flags.at[0]), (ku, flags.at[1])]
+            [(od, od_v), (ou, ou_v), (master.at[:, columns(h)], master_v.at[:, columns(h)]),
+             (tok, a_all.at[me]), (fd, fd_v), (og, og_v), (fu, fu_v), (md, old_moments.at[0]), (vd, old_moments.at[1]),
+             (mu, old_moments.at[2]), (vu, old_moments.at[3]), (kd, flags.at[0]), (ku, flags.at[1]),
+             (master.at[:, columns(other)], master_v.at[:, columns(other)])]
         )
     ]
     for load in loads:
         load.start()
     barrier = pltpu.get_barrier_semaphore()
+    for d in (1, -1):
+        pl.semaphore_signal(barrier, inc=1, device_id=ring(d), device_id_type=MESH)
 
     def greet_plane(d, carry):
         pl.semaphore_signal(barrier, inc=1, device_id=plane(lax.rem(me + d, 2 * NC)), device_id_type=MESH)
         return carry
 
-    def greet_ring(d, carry):
-        pl.semaphore_signal(barrier, inc=1, device_id=ring(d), device_id_type=MESH)
-        return carry
-
     lax.fori_loop(1, 2 * NC, greet_plane, 0)
-    greet_ring(1, 0)
-    greet_ring(-1, 0)
 
     for load in loads[:3]:
         load.wait()
 
     def merge(half):
-        cols = pl.ds(pl.multiple_of(half * 256, 256), 256)
+        cols = columns(half)
         both = master_v[:, cols] + adapter_scale * split3(od_v[...], ou_v[:, cols])
         merged_v[:, cols] = both
         w_v[:, cols] = both.astype(BF16)
         return both.astype(BF16)
 
     b_all[z] = merge(h)
+    pl.semaphore_wait(barrier, 2 * NC - 1 + 2)
+
+    def tell(i, distance):
+        for d in (distance, -distance):
+            pl.semaphore_signal(far_sem.at[i], inc=1, device_id=ring(d), device_id_type=MESH)
+
+    def told(i):
+        pl.semaphore_wait(far_sem.at[i], 2)
+
+    def chunk(zz, q):
+        return b_all.at[zz, pl.ds((q % 2) * 256, 256), pl.ds((q // 2) * 128, 128)]
+
+    def b_out(direction, step, q):
+        sign = 1 if direction == 0 else -1
+        origin = ring(-sign * (step - 1))[0]
+        send(chunk(origin, q), chunk(origin, q), b_send, b_recv.at[direction, step - 1, q], ring(sign))
+
+    def b_in(direction, step, q):
+        sign = 1 if direction == 0 else -1
+        origin = ring(-sign * step)[0]
+        arrived(chunk(origin, q), b_recv.at[direction, step - 1, q])
+
+    for q in range(4):
+        for direction in (0, 1):
+            b_out(direction, 1, q)
+
+    tell(0, 1)
 
     for load in loads[3:7]:
         load.wait()
@@ -131,41 +158,6 @@
         og_v[...], up_cast, (((1,), (1,)), ((), ())), preferred_element_type=F32
     )
     part[:, :, 128:256] = backward.reshape(NC, 16, 128)
-    merge(other)
-    stores = [
-        pltpu.make_async_copy(merged_v, merged, st_sem.at[2]),
-        pltpu.make_async_copy(w_v, w, st_sem.at[3]),
-    ]
-    for store in stores:
-        store.start()
-
-    pl.semaphore_wait(barrier, 2 * NC - 1 + 2)
-
-    def tell(i, distance):
-        for d in (distance, -distance):
-            pl.semaphore_signal(far_sem.at[i], inc=1, device_id=ring(d), device_id_type=MESH)
-
-    def told(i):
-        pl.semaphore_wait(far_sem.at[i], 2)
-
-    tell(0, 1)
-
-    def chunk(zz, q):
-        return b_all.at[zz, pl.ds((q % 2) * 256, 256), pl.ds((q // 2) * 128, 128)]
-
-    def b_out(direction, step, q):
-        sign = 1 if direction == 0 else -1
-        origin = ring(-sign * (step - 1))[0]
-        send(chunk(origin, q), chunk(origin, q), b_send, b_recv.at[direction, step - 1, q], ring(sign))
-
-    def b_in(direction, step, q):
-        sign = 1 if direction == 0 else -1
-        origin = ring(-sign * step)[0]
-        arrived(chunk(origin, q), b_recv.at[direction, step - 1, q])
-
-    for q in range(4):
-        for direction in (0, 1):
-            b_out(direction, 1, q)
 
     def rs_out(d, carry):
         to = lax.rem(c + d, NC)
@@ -228,6 +220,15 @@
     for half in (0, 1):
         p2_own(half, 0)
 
+    loads[13].wait()
+    merge(other)
+    stores = [
+        pltpu.make_async_copy(merged_v, merged, st_sem.at[2]),
+        pltpu.make_async_copy(w_v, w, st_sem.at[3]),
+    ]
+    for store in stores:
+        store.start()
+
     def sum_rows():
         arrived(rs, rs_recv)
         total = part[c]
@@ -246,8 +247,7 @@
 
     def start_outputs():
         arrived(hb_all.at[pl.ds(0, 2 * NC - 1)], hb_recv)
-        cols = pl.ds(pl.multiple_of(h * 256, 256), 256)
-        up_half = fu_v[:, cols].astype(BF16)
+        up_half = fu_v[:, columns(h)].astype(BF16)
         for hp in (0, 1):
             acc[hp] = adapter_scale * jnp.dot(rows_of(hp)[:, :128], up_half, preferred_element_type=F32)
 
@@ -288,7 +288,7 @@
 
     def end_gradients():
         arrived(gbuf.at[other], gx_sem.at[1])
-        for load in loads[7:]:
+        for load in loads[7:13]:
             load.wait()
         for u in (0, 1):
             for hp in (0, 1):
@@ -335,26 +335,25 @@
 
     after = {
         0: [doubling],
-        1: [sum_rows],
         2: [doubled],
-        3: [p1_near],
-        5: [p1_far, start_outputs, up_gradient],
+        3: [sum_rows],
+        4: [p1_near],
         6: [lambda: p2_near(1, 0), lambda: p2_near(0, 0)],
-        8: [lambda: p2_far(1, 0), lambda: p2_far(0, 0), gradients],
-        10: [lambda: p2_near(0, 3), lambda: p2_near(1, 3)],
-        11: [lambda: p2_near(0, 1), lambda: p2_near(1, 1)],
-        12: [lambda: p2_near(0, 2), lambda: p2_near(1, 2)],
-        14: [lambda: p2_far(0, 3), lambda: p2_far(1, 3)],
-        15: [lambda: p2_far(0, 1), lambda: p2_far(1, 1)],
-        16: [lambda: p2_far(0, 2), lambda: p2_far(1, 2)],
-        17: [sum_gradients],
-        19: [first_products],
-        20: [lambda: products(2, 2), end_gradients],
-        21: [lambda: products(3, 3)],
-        22: [lambda: products(4, 4)],
-        23: [lambda: products(5, 5)],
-        24: [lambda: products(6, 6)],
-        27: [lambda: products(7, 7)],
+        7: [p1_far],
+        10: [start_outputs, up_gradient],
+        11: [lambda: p2_near(0, 3), lambda: p2_near(1, 3)],
+        12: [lambda: p2_near(0, 1), lambda: p2_near(1, 1), lambda: p2_far(1, 0)],
+        13: [lambda: p2_far(0, 0)],
+        14: [gradients],
+        15: [lambda: p2_near(0, 2), lambda: p2_near(1, 2)],
+        18: [lambda: p2_far(0, 3), lambda: p2_far(1, 3)],
+        19: [lambda: p2_far(0, 1), lambda: p2_far(1, 1)],
+        20: [lambda: p2_far(0, 2), lambda: p2_far(1, 2)],
+        22: [first_products],
+        23: [sum_gradients, lambda: products(2, 3)],
+        24: [lambda: products(4, 5)],
+        25: [lambda: products(6, 6)],
+        27: [lambda: products(7, 7), end_gradients],
     }
     for tick in range(28):
         step, q = tick // 4 + 1, tick % 4
@@ -462,7 +461,7 @@
             vmem((2, 2, 256, 128), BF16),
             vmem((4, 32, 128), F32),
             pltpu.SMEM((2, 2), jnp.int32),
-            dma((13,)),
+            dma((14,)),
             dma((5,)),
             dma,
             dma((2, 8, 4)),

time: 82.6 us -> 73.3 us (0.89)
  Pallas kernels: 81.8 us -> 72.5 us
    pallas_call x1, Pallas kernels: 79.4 us -> 70.1 us  [body(): pl.pallas_call(kernel, out_shape=(jax.ShapeDtypeStruct((512, 512), F32),...]
where the time goes in v3:
time: 73.3 us; the launch traced here: 73.1 us
  Pallas kernels  72.5 us (99%)
    pallas_call x1, Pallas kernels, body(): pl.pallas_call(kernel, out_shape=(jax.ShapeDtypeStruct((512, 512), F32),...  70.1 us
    pallas_call x1, Pallas kernels, body(): pl.pallas_call(write_out, out_shape=(jax.ShapeDtypeStruct((512, 512), F32...  2.42 us

profile of v3, /device:TPU:1, one launch (start us, length us, event | category | flops | bytes accessed | tf_op | source)
XLA Modules:
  0.0 73.1 jit_solution(1621138389321312636)
XLA Ops:
  0.6 70.1 %relora_step.1 = (f32[512,512]{1,0:T(8,128)}, bf16[512,512]{1,0:T(8,128)(2,1)}, bf16[256,512]{1,0:T(8,128)(2,1)}, f32[4,32,128]{2,1,0:T(8,128)}) custom-call(bf16[256,512]{1,0:T(8,128)(2,1)} %tok.1, bf16[256,512]{1,0:T(8,128)(2,1)} %og.1, f32[512,512]{1,0:T(8,128)} %master.1, f32[512,128]{1,0:T(8,128)} %od.1, f32[128,512]{1,0:T(8,128)} %ou.1, ...), custom_call_target="tpu_custom_call" | custom-call | tf_op jit(solution)/shard_map/relora_step/pallas_call | solution.py:428
  70.7 2.4 %write_out.1 = (f32[512,512]{1,0:T(8,128)}, bf16[512,512]{1,0:T(8,128)(2,1)}, bf16[256,512]{1,0:T(8,128)(2,1)}, f32[32,128]{1,0:T(8,128)}, f32[32,128]{1,0:T(8,1...) custom-call(f32[512,512]{1,0:T(8,128)} %get-tuple-element.18.merged, bf16[512,512]{1,0:T(8,128)(2,1)} %get-tuple-element.19.w, ...), custom_call_target="tpu_custom_call" | custom-call | tf_op jit(solution)/shard_map/write_out/pallas_call | solution.py:493

commit v4 on v3

--- a/solution.py
+++ b/solution.py
@@ -34,9 +34,9 @@
     tok, og, master, od, ou, fd, fu, md, vd, mu, vu, kd, ku,
     merged, w, out, moments,
     a_all, b_all, og_v, master_v, merged_v, w_v, moments_v, od_v, ou_v, fd_v, fu_v,
-    part, rs, hb_all, gtmp, up_send, up_recv, gsum, gsend, grecv, gbuf, acc, stage, old_moments, flags,
+    part, rs, hb_all, gtmp, up_send, up_recv, gsum, pair_send, pair_recv, gsend, grecv, gbuf, acc, stage, old_moments, flags,
     ld_sem, st_sem, b_send, b_recv, p1_recv, p2_recv, c_recv, a_send,
-    rs_send, rs_recv, hb_send, hb_recv, up_sem, g_send, g_recv, gx_sem, o_send, o_recv, far_sem,
+    rs_send, rs_recv, hb_send, hb_recv, up_sem, pair_sem, g_send, g_recv, gx_sem, o_send, o_recv, far_sem,
 ):
     z = lax.axis_index("row")
     c = lax.axis_index("col")
@@ -251,37 +251,51 @@
         for hp in (0, 1):
             acc[hp] = adapter_scale * jnp.dot(rows_of(hp)[:, :128], up_half, preferred_element_type=F32)
 
+    parity = lax.rem(z, 2)
+    toward = lax.select(parity == core, 1, -1)
+
+    def kept(u, gradient):
+        gtmp[...] = (adapter_scale * gradient).reshape(NZ, 2, 16, 128)
+        rows = gtmp[:, h].reshape(NZ // 2, 2, 16, 128)
+        for p in (0, 1):
+            gsum[p, :, u] = rows[:, p]
+
     def up_gradient():
         up = contract_rows(og_v[...], hb_all[pl.ds(h * NC, NC)].reshape(256, 256)[:, :128])
-        gtmp[...] = (adapter_scale * up).reshape(NZ, 2, 16, 128)
+        kept(1, up)
         up_send[...] = gtmp[:, other].astype(BF16)
-        gsum[1] = gtmp[:, h]
         send(up_send, up_recv, up_sem.at[0], up_sem.at[1], partner_rep)
 
     def gradients():
         down = jnp.zeros((512, 128), F32)
         for hp in (0, 1):
             down = down + contract_rows(a_all[hp * NC + c], rows_of(hp)[:, 128:])
-        gtmp[...] = (adapter_scale * down).reshape(NZ, 2, 16, 128)
-        gsum[0] = gtmp[:, h]
+        kept(0, down)
         arrived(up_recv, up_sem.at[1])
-        gsum[1] += up_recv[...].astype(F32)
-        for u in (0, 1):
-            gsend[:, u] = gsum[u].astype(BF16)
+        rows = up_recv[...].astype(F32).reshape(NZ // 2, 2, 16, 128)
+        for p in (0, 1):
+            gsum[p, :, 1] += rows[:, p]
+        pair_send[...] = gsum[1 - parity].astype(BF16)
+        send(pair_send, pair_recv, pair_sem.at[0], pair_sem.at[1], ring(toward))
+
+    def pair_gradients():
+        arrived(pair_recv, pair_sem.at[1])
+        gsum[parity] += pair_recv[...].astype(F32)
+        gsend[...] = gsum[parity].astype(BF16)
         told(2)
 
         def g_out(d, carry):
-            to = lax.rem(z + d, NZ)
-            send(gsend.at[to], grecv.at[d - 1], g_send, g_recv, (to, c, h))
+            to = lax.rem(z + 2 * d, NZ)
+            send(gsend.at[lax.div(to, 2)], grecv.at[d - 1], g_send, g_recv, (to, c, h))
             return carry
 
-        lax.fori_loop(1, NZ, g_out, 0)
+        lax.fori_loop(1, NZ // 2, g_out, 0)
 
     def sum_gradients():
         arrived(grecv, g_recv)
         for u in (0, 1):
-            total = gsum[u, z]
-            for d in range(NZ - 1):
+            total = gsum[parity, lax.div(z, 2), u]
+            for d in range(NZ // 2 - 1):
                 total = total + grecv[d, u].astype(F32)
             gbuf[h, u] = total
         send(gbuf.at[h], gbuf.at[h], gx_sem.at[0], gx_sem.at[1], partner_rep)
@@ -347,13 +361,13 @@
         14: [gradients],
         15: [lambda: p2_near(0, 2), lambda: p2_near(1, 2)],
         18: [lambda: p2_far(0, 3), lambda: p2_far(1, 3)],
-        19: [lambda: p2_far(0, 1), lambda: p2_far(1, 1)],
+        19: [pair_gradients, lambda: p2_far(0, 1), lambda: p2_far(1, 1)],
         20: [lambda: p2_far(0, 2), lambda: p2_far(1, 2)],
         22: [first_products],
-        23: [sum_gradients, lambda: products(2, 3)],
+        23: [lambda: products(2, 3)],
         24: [lambda: products(4, 5)],
         25: [lambda: products(6, 6)],
-        27: [lambda: products(7, 7), end_gradients],
+        27: [lambda: products(7, 7), sum_gradients],
     }
     for tick in range(28):
         step, q = tick // 4 + 1, tick % 4
@@ -383,6 +397,7 @@
                 keep.start()
                 stores.append(keep)
 
+    end_gradients()
     for store in stores:
         store.wait()
     sent(a_all.at[pl.ds(0, 31)], a_send)
@@ -390,6 +405,7 @@
     sent(rs, rs_send)
     sent(hb_all.at[pl.ds(0, 2 * NC - 1)], hb_send)
     sent(up_send, up_sem.at[0])
+    sent(pair_send, pair_sem.at[0])
     sent(grecv, g_send)
     sent(gbuf.at[h], gx_sem.at[0])
     for part_of in (0, 1):
@@ -453,9 +469,11 @@
             vmem((NZ, 2, 16, 128), F32),
             vmem((NZ, 16, 128), BF16),
             vmem((NZ, 16, 128), BF16),
-            vmem((2, NZ, 16, 128), F32),
-            vmem((NZ, 2, 16, 128), BF16),
-            vmem((NZ - 1, 2, 16, 128), BF16),
+            vmem((2, NZ // 2, 2, 16, 128), F32),
+            vmem((NZ // 2, 2, 16, 128), BF16),
+            vmem((NZ // 2, 2, 16, 128), BF16),
+            vmem((NZ // 2, 2, 16, 128), BF16),
+            vmem((NZ // 2 - 1, 2, 16, 128), BF16),
             vmem((2, 2, 16, 128), F32),
             vmem((2, 256, 256), F32),
             vmem((2, 2, 256, 128), BF16),
@@ -473,6 +491,7 @@
             dma,
             dma,
             dma,
+            dma((2,)),
             dma((2,)),
             dma,
             dma,

time: 73.3 us -> 71.4 us (0.974)
  Pallas kernels: 72.5 us -> 70.4 us
    pallas_call x1, Pallas kernels: 70.1 us -> 68 us  [body(): pl.pallas_call(kernel, out_shape=(jax.ShapeDtypeStruct((512, 512), F32),...]
where the time goes in v4:
time: 71.4 us; the launch traced here: 71 us
  Pallas kernels  70.4 us (99%)
    pallas_call x1, Pallas kernels, body(): pl.pallas_call(kernel, out_shape=(jax.ShapeDtypeStruct((512, 512), F32),...  68 us
    pallas_call x1, Pallas kernels, body(): pl.pallas_call(write_out, out_shape=(jax.ShapeDtypeStruct((512, 512), F32...  2.42 us

profile of v4, /device:TPU:1, one launch (start us, length us, event | category | flops | bytes accessed | tf_op | source)
XLA Modules:
  0.0 71.0 jit_solution(5140970756266258900)
XLA Ops:
  0.6 68.0 %relora_step.1 = (f32[512,512]{1,0:T(8,128)}, bf16[512,512]{1,0:T(8,128)(2,1)}, bf16[256,512]{1,0:T(8,128)(2,1)}, f32[4,32,128]{2,1,0:T(8,128)}) custom-call(bf16[256,512]{1,0:T(8,128)(2,1)} %tok.1, bf16[256,512]{1,0:T(8,128)(2,1)} %og.1, f32[512,512]{1,0:T(8,128)} %master.1, f32[512,128]{1,0:T(8,128)} %od.1, f32[128,512]{1,0:T(8,128)} %ou.1, ...), custom_call_target="tpu_custom_call" | custom-call | tf_op jit(solution)/shard_map/relora_step/pallas_call | solution.py:444
  68.6 2.4 %write_out.1 = (f32[512,512]{1,0:T(8,128)}, bf16[512,512]{1,0:T(8,128)(2,1)}, bf16[256,512]{1,0:T(8,128)(2,1)}, f32[32,128]{1,0:T(8,128)}, f32[32,128]{1,0:T(8,1...) custom-call(f32[512,512]{1,0:T(8,128)} %get-tuple-element.18.merged, bf16[512,512]{1,0:T(8,128)(2,1)} %get-tuple-element.19.w, ...), custom_call_target="tpu_custom_call" | custom-call | tf_op jit(solution)/shard_map/write_out/pallas_call | solution.py:512

commit v5 on v4

--- a/solution.py
+++ b/solution.py
@@ -36,7 +36,7 @@
     a_all, b_all, og_v, master_v, merged_v, w_v, moments_v, od_v, ou_v, fd_v, fu_v,
     part, rs, hb_all, gtmp, up_send, up_recv, gsum, pair_send, pair_recv, gsend, grecv, gbuf, acc, stage, old_moments, flags,
     ld_sem, st_sem, b_send, b_recv, p1_recv, p2_recv, c_recv, a_send,
-    rs_send, rs_recv, hb_send, hb_recv, up_sem, pair_sem, g_send, g_recv, gx_sem, o_send, o_recv, far_sem,
+    rs_send, rs_recv, hb_send, hb_recv, up_sem, pair_sem, g_send, g_recv, gx_sem, o_send, o_recv, far_sem, b_last,
 ):
     z = lax.axis_index("row")
     c = lax.axis_index("col")
@@ -132,10 +132,10 @@
     def chunk(zz, q):
         return b_all.at[zz, pl.ds((q % 2) * 256, 256), pl.ds((q // 2) * 128, 128)]
 
-    def b_out(direction, step, q):
+    def b_out(direction, step, q, send_sem=b_send):
         sign = 1 if direction == 0 else -1
         origin = ring(-sign * (step - 1))[0]
-        send(chunk(origin, q), chunk(origin, q), b_send, b_recv.at[direction, step - 1, q], ring(sign))
+        send(chunk(origin, q), chunk(origin, q), send_sem, b_recv.at[direction, step - 1, q], ring(sign))
 
     def b_in(direction, step, q):
         sign = 1 if direction == 0 else -1
@@ -373,16 +373,23 @@
         step, q = tick // 4 + 1, tick % 4
         for direction in (0, 1):
             b_in(direction, step, q)
-            if step < 7 or q % 2 == direction:
+            if step < 7:
                 b_out(direction, step + 1, q)
+            elif q % 2 == 1 and direction == 1:
+                b_out(1, 8, q, b_last.at[0])
+            elif q % 2 == 0 and direction == 0:
+                pl.when(z < NZ - 1)(lambda q=q: b_out(0, 8, q, b_last.at[1]))
+            elif q % 2 == 0 and direction == 1:
+                pl.when(z == 1)(lambda q=q: b_out(1, 8, q, b_last.at[2]))
         for action in after.get(tick, ()):
             action()
 
     far = lax.rem(z + 8, NZ)
     outs = []
     for part_of in (0, 1):
-        for direction in (0, 1):
-            b_in(direction, 8, 2 * part_of + direction)
+        pl.when(z > 0)(lambda q=2 * part_of: b_in(0, 8, q))
+        pl.when(z == 0)(lambda q=2 * part_of: b_in(1, 8, q))
+        b_in(1, 8, 2 * part_of + 1)
         cols = pl.ds(part_of * 128, 128)
         there = pl.ds(pl.multiple_of(h * 256 + part_of * 128, 128), 128)
         for hp in (other, h):
@@ -401,7 +408,11 @@
     for store in stores:
         store.wait()
     sent(a_all.at[pl.ds(0, 31)], a_send)
-    sent(b_all.at[pl.ds(0, 15)], b_send)
+    sent(b_all.at[pl.ds(0, 14)], b_send)
+    two = b_all.at[0, pl.ds(0, 256)]
+    sent(two, b_last.at[0])
+    pl.when(z < NZ - 1)(lambda: sent(two, b_last.at[1]))
+    pl.when(z == 1)(lambda: sent(two, b_last.at[2]))
     sent(rs, rs_send)
     sent(hb_all.at[pl.ds(0, 2 * NC - 1)], hb_send)
     sent(up_send, up_sem.at[0])
@@ -499,6 +510,7 @@
             dma((2,)),
             dma((2,)),
             pltpu.SemaphoreType.REGULAR((3,)),
+            dma((3,)),
         ],
         compiler_params=pltpu.CompilerParams(
             collective_id=0, has_side_effects=True, vmem_limit_bytes=60 * 1024 * 1024

time: 71.4 us -> 70.3 us (0.985)
  Pallas kernels: 70.4 us -> 69.4 us
    pallas_call x1, Pallas kernels: 68 us -> 67 us  [body(): pl.pallas_call(kernel, out_shape=(jax.ShapeDtypeStruct((512, 512), F32),...]
where the time goes in v5:
time: 70.3 us; the launch traced here: 70.1 us
  Pallas kernels  69.4 us (99%)
    pallas_call x1, Pallas kernels, body(): pl.pallas_call(kernel, out_shape=(jax.ShapeDtypeStruct((512, 512), F32),...  67 us
    pallas_call x1, Pallas kernels, body(): pl.pallas_call(write_out, out_shape=(jax.ShapeDtypeStruct((512, 512), F32...  2.42 us

profile of v5, /device:TPU:1, one launch (start us, length us, event | category | flops | bytes accessed | tf_op | source)
XLA Modules:
  0.0 70.1 jit_solution(3768412270377744771)
XLA Ops:
  0.6 67.0 %relora_step.1 = (f32[512,512]{1,0:T(8,128)}, bf16[512,512]{1,0:T(8,128)(2,1)}, bf16[256,512]{1,0:T(8,128)(2,1)}, f32[4,32,128]{2,1,0:T(8,128)}) custom-call(bf16[256,512]{1,0:T(8,128)(2,1)} %tok.1, bf16[256,512]{1,0:T(8,128)(2,1)} %og.1, f32[512,512]{1,0:T(8,128)} %master.1, f32[512,128]{1,0:T(8,128)} %od.1, f32[128,512]{1,0:T(8,128)} %ou.1, ...), custom_call_target="tpu_custom_call" | custom-call | tf_op jit(solution)/shard_map/relora_step/pallas_call | solution.py:455
  67.7 2.4 %write_out.1 = (f32[512,512]{1,0:T(8,128)}, bf16[512,512]{1,0:T(8,128)(2,1)}, bf16[256,512]{1,0:T(8,128)(2,1)}, f32[32,128]{1,0:T(8,128)}, f32[32,128]{1,0:T(8,1...) custom-call(f32[512,512]{1,0:T(8,128)} %get-tuple-element.18.merged, bf16[512,512]{1,0:T(8,128)(2,1)} %get-tuple-element.19.w, ...), custom_call_target="tpu_custom_call" | custom-call | tf_op jit(solution)/shard_map/write_out/pallas_call | solution.py:524

commit v6 on v5

--- a/solution.py
+++ b/solution.py
@@ -97,7 +97,7 @@
              (master.at[:, columns(other)], master_v.at[:, columns(other)])]
         )
     ]
-    for load in loads:
+    for load in loads[:3]:
         load.start()
     barrier = pltpu.get_barrier_semaphore()
     for d in (1, -1):
@@ -108,18 +108,20 @@
         return carry
 
     lax.fori_loop(1, 2 * NC, greet_plane, 0)
+    for load in loads[3:]:
+        load.start()
 
     for load in loads[:3]:
         load.wait()
 
-    def merge(half):
-        cols = columns(half)
+    def merge(first, length):
+        cols = pl.ds(pl.multiple_of(first, 128), length)
         both = master_v[:, cols] + adapter_scale * split3(od_v[...], ou_v[:, cols])
         merged_v[:, cols] = both
         w_v[:, cols] = both.astype(BF16)
         return both.astype(BF16)
 
-    b_all[z] = merge(h)
+    b_all[z, :, 0:128] = merge(h * 256, 128)
     pl.semaphore_wait(barrier, 2 * NC - 1 + 2)
 
     def tell(i, distance):
@@ -143,6 +145,8 @@
         arrived(chunk(origin, q), b_recv.at[direction, step - 1, q])
 
     for q in range(4):
+        if q == 2:
+            b_all[z, :, 128:256] = merge(h * 256 + 128, 128)
         for direction in (0, 1):
             b_out(direction, 1, q)
 
@@ -221,7 +225,7 @@
         p2_own(half, 0)
 
     loads[13].wait()
-    merge(other)
+    merge(other * 256, 256)
     stores = [
         pltpu.make_async_copy(merged_v, merged, st_sem.at[2]),
         pltpu.make_async_copy(w_v, w, st_sem.at[3]),

time: 70.3 us -> 70.2 us (level); the launches traced: 70.1 us -> 69.2 us
  Pallas kernels: 69.4 us -> 68.5 us
    pallas_call x1, Pallas kernels: 67 us -> 66.1 us  [body(): pl.pallas_call(kernel, out_shape=(jax.ShapeDtypeStruct((512, 512), F32),...]
where the time goes in v6:
time: 70.2 us; the launch traced here: 69.2 us
  Pallas kernels  68.5 us (98%)
    pallas_call x1, Pallas kernels, body(): pl.pallas_call(kernel, out_shape=(jax.ShapeDtypeStruct((512, 512), F32),...  66.1 us
    pallas_call x1, Pallas kernels, body(): pl.pallas_call(write_out, out_shape=(jax.ShapeDtypeStruct((512, 512), F32...  2.42 us

profile of v6, /device:TPU:1, one launch (start us, length us, event | category | flops | bytes accessed | tf_op | source)
XLA Modules:
  0.0 69.2 jit_solution(11083326859465875902)
XLA Ops:
  0.6 66.1 %relora_step.1 = (f32[512,512]{1,0:T(8,128)}, bf16[512,512]{1,0:T(8,128)(2,1)}, bf16[256,512]{1,0:T(8,128)(2,1)}, f32[4,32,128]{2,1,0:T(8,128)}) custom-call(bf16[256,512]{1,0:T(8,128)(2,1)} %tok.1, bf16[256,512]{1,0:T(8,128)(2,1)} %og.1, f32[512,512]{1,0:T(8,128)} %master.1, f32[512,128]{1,0:T(8,128)} %od.1, f32[128,512]{1,0:T(8,128)} %ou.1, ...), custom_call_target="tpu_custom_call" | custom-call | tf_op jit(solution)/shard_map/relora_step/pallas_call | solution.py:459
  66.8 2.4 %write_out.1 = (f32[512,512]{1,0:T(8,128)}, bf16[512,512]{1,0:T(8,128)(2,1)}, bf16[256,512]{1,0:T(8,128)(2,1)}, f32[32,128]{1,0:T(8,128)}, f32[32,128]{1,0:T(8,1...) custom-call(f32[512,512]{1,0:T(8,128)} %get-tuple-element.18.merged, bf16[512,512]{1,0:T(8,128)(2,1)} %get-tuple-element.19.w, ...), custom_call_target="tpu_custom_call" | custom-call | tf_op jit(solution)/shard_map/write_out/pallas_call | solution.py:528
